TPU v7x, 32 devices: a whole 2x2x4 slice. The times are simulated.
32 devices in a mesh: rows: 16 (over z, x, core), cols: 2 (over y).
Axes of the slice: x: 2, y: 2, z: 4, core: 2. Of those that a mesh axis runs over, the one named last changes fastest.
Arguments:
- frames_in: bfloat16 [3, 96, 16, 256], P(None, 'rows', 'cols'), may hold values from -6 to 6
- cotangent: bfloat16 [3, 96, 16, 256], P(None, 'rows', 'cols'), may hold values from -6 to 6
- core: float32 [110592], P(('rows', 'cols')), may hold values from -0.3 to 0.3
- moment_one: float32 [110592], P(('rows', 'cols')), may hold values from -0.6 to 0.6
- moment_two: float32 [110592], P(('rows', 'cols')), may hold values from 0.01 to 0.16
- u_in: bfloat16 [256, 64], replicated, may hold values from -0.375 to 0.375
- u_out: bfloat16 [256, 64], replicated, may hold values from -0.375 to 0.375
Outputs:
- frames_grad: bfloat16 [3, 96, 16, 256], P(None, 'rows', 'cols')
- core_next: float32 [110592], P(('rows', 'cols'))
- moment_one_next: float32 [110592], P(('rows', 'cols'))
- moment_two_next: float32 [110592], P(('rows', 'cols'))
- kernel_next: bfloat16 [27, 256, 256], replicated
All inputs are finite; a program needn't handle non-finite values.
Results may differ from a plain program's by a relative error of at most 0.014.
Values may be sent and summed in bfloat16 or wider, within the bound.
A program may use at most 64 MiB of HBM per device.

v0:
```python
import functools
import math

import jax
import jax.numpy as jnp
from jax import lax
from jax.experimental import pallas as pl
from jax.experimental.pallas import tpu as pltpu
from jax.sharding import PartitionSpec as P

beta_one = 0.9
beta_two = 0.999
learn_rate = 0.06
epsilon = 1e-08
fix_one = 1.0 - 0.9**10
fix_two = 1.0 - 0.999**10


def extended(block, sides, width):
    for axis, dim in sides:
        count = lax.axis_size(axis)
        forward = [(i, i + 1) for i in range(count - 1)]
        backward = [(target, source) for source, target in forward]
        low = lax.ppermute(
            lax.slice_in_dim(block, block.shape[dim] - width, None, axis=dim), axis, forward
        )
        high = lax.ppermute(lax.slice_in_dim(block, 0, width, axis=dim), axis, backward)
        block = jnp.concatenate([low, block, high], axis=dim)
    return block


def build(flat_core, u_in, u_out):
    rank = u_in.shape[1]
    cube = flat_core.reshape(-1, rank).astype(jnp.bfloat16)
    halfway = lax.dot_general(
        cube, u_out, (((1,), (1,)), ((), ())), preferred_element_type=jnp.float32
    ).astype(jnp.bfloat16)
    halfway = halfway.reshape(-1, rank, u_out.shape[0])
    kernel = jnp.einsum("ip,tpo->tio", u_in, halfway, preferred_element_type=jnp.float32)
    return kernel.astype(jnp.bfloat16)


def offsets():
    return [(a, b, c) for a in range(3) for b in range(3) for c in range(3)]


def forward_sum(padded, kernel, frames, rows, cols):
    chans = padded.shape[3]
    total = jnp.zeros((frames * rows * cols, kernel.shape[2]), jnp.float32)
    for tap, (a, b, c) in enumerate(offsets()):
        piece = padded[a : a + frames, b : b + rows, c : c + cols, :].reshape(-1, chans)
        total = total + jnp.dot(piece, kernel[tap], preferred_element_type=jnp.float32)
    return total.reshape(frames, rows, cols, -1)


def backward_sum(padded, kernel, frames, rows, cols):
    chans = padded.shape[3]
    total = jnp.zeros((frames * rows * cols, kernel.shape[1]), jnp.float32)
    for tap, (a, b, c) in enumerate(offsets()):
        piece = padded[
            2 - a : 2 - a + frames, 2 - b : 2 - b + rows, 2 - c : 2 - c + cols, :
        ].reshape(-1, chans)
        total = total + lax.dot_general(
            piece, kernel[tap], (((1,), (1,)), ((), ())), preferred_element_type=jnp.float32
        )
    return total.reshape(frames, rows, cols, -1)


def core_terms(padded, slope, u_in, u_out, frames, rows, cols):
    chans = padded.shape[3]
    shape_pad = padded.shape
    in_proj = jnp.dot(padded.reshape(-1, chans), u_in, preferred_element_type=jnp.float32).astype(
        jnp.bfloat16
    )
    in_proj = in_proj.reshape(shape_pad[0], shape_pad[1], shape_pad[2], -1)
    out_proj = jnp.dot(slope.reshape(-1, chans), u_out, preferred_element_type=jnp.float32).astype(
        jnp.bfloat16
    )
    grads = []
    for tap, (a, b, c) in enumerate(offsets()):
        piece = in_proj[a : a + frames, b : b + rows, c : c + cols, :].reshape(-1, in_proj.shape[3])
        grads.append(
            lax.dot_general(
                piece, out_proj, (((0,), (0,)), ((), ())), preferred_element_type=jnp.float32
            )
        )
    return jnp.stack(grads).reshape(-1)


def time_pad(tile):
    return jnp.pad(tile, ((1, 1), (0, 0), (0, 0), (0, 0)))


def slope_of(cotangent, pre):
    sig = jax.nn.sigmoid(pre)
    return (cotangent.astype(jnp.float32) * sig * (1.0 + pre * (1.0 - sig))).astype(jnp.bfloat16)


def plain_body(frames_in, cotangent, core, moment_one, moment_two, u_in, u_out):
    frames, rows, cols = (frames_in.shape[0], frames_in.shape[1], frames_in.shape[2])
    whole_core = lax.all_gather(core, ("rows", "cols"), axis=0, tiled=True)
    kernel = build(whole_core, u_in, u_out)
    rimmed = extended(frames_in, (("rows", 1), ("cols", 2)), 1)
    padded = time_pad(rimmed)
    pre = forward_sum(padded, kernel, frames, rows, cols)
    slope = slope_of(cotangent, pre)
    slope_rimmed = extended(slope, (("rows", 1), ("cols", 2)), 1)
    slope_pad = time_pad(slope_rimmed)
    frames_grad = backward_sum(slope_pad, kernel, frames, rows, cols).astype(jnp.bfloat16)
    local_grad = core_terms(padded, slope, u_in, u_out, frames, rows, cols)
    partial_grad = lax.psum_scatter(
        local_grad.astype(jnp.bfloat16), "rows", scatter_dimension=0, tiled=True
    ).astype(jnp.float32)
    core_grad = lax.psum_scatter(partial_grad, "cols", scatter_dimension=0, tiled=True)
    cells = frames * rows * lax.axis_size("rows") * cols * lax.axis_size("cols")
    core_grad = core_grad / math.sqrt(cells)
    moment_one_next = beta_one * moment_one + (1.0 - beta_one) * core_grad
    moment_two_next = beta_two * moment_two + (1.0 - beta_two) * core_grad * core_grad
    core_next = core - learn_rate * (moment_one_next / fix_one) / (
        jnp.sqrt(moment_two_next / fix_two) + epsilon
    )
    new_whole = lax.all_gather(core_next, ("rows", "cols"), axis=0, tiled=True)
    kernel_next = build(new_whole, u_in, u_out)
    return (frames_grad, core_next, moment_one_next, moment_two_next, kernel_next)


MESH = pl.DeviceIdType.MESH
vmem_limit = 67043328
NEIGHBOURS = [(dr, dc) for dr in (-1, 0, 1) for dc in (-1, 0, 1) if (dr, dc) != (0, 0)]


def dot(a, b, dims):
    return lax.dot_general(a, b, (dims, ((), ())), preferred_element_type=jnp.float32)


def pair_matrix(rank):
    row = lax.broadcasted_iota(jnp.int32, (rank, rank), 0)
    col = lax.broadcasted_iota(jnp.int32, (rank, rank), 1)
    half = rank // 2
    source = jnp.where(row < half, 2 * row, 2 * (row - half) + 1)
    return jnp.where(col == source, 1.0, 0.0).astype(jnp.bfloat16)


def shifted(wide, c):
    _, frames, rows, cols, rank = wide.shape
    count = frames * rows * cols
    own = wide[1].reshape(count, rank)
    if c == 1:
        return own
    col = lax.broadcasted_iota(jnp.int32, (count, rank), 0) % cols
    if c == 0:
        side = wide[0].reshape(count, rank)
        return jnp.where(
            col == 0, pltpu.roll(side, count - (cols - 1), 0), pltpu.roll(own, 1, 0)
        )
    side = wide[2].reshape(count, rank)
    return jnp.where(
        col == cols - 1, pltpu.roll(side, cols - 1, 0), pltpu.roll(own, count - 1, 0)
    )


def fill_taps(wide, out, flip):
    _, frames, rows, cols, rank = wide.shape
    cells = (frames - 2) * (rows - 2) * cols
    moved = [
        shifted(wide, c).reshape(frames, rows, cols, rank) for c in range(3)
    ]
    for tap, (a, b, c) in enumerate(offsets()):
        if flip:
            a, b, c = 2 - a, 2 - b, 2 - c
        piece = moved[c][a : a + frames - 2, b : b + rows - 2].reshape(cells, rank)
        out[:, rank * tap : rank * (tap + 1)] = piece.astype(jnp.bfloat16)


def cube_rows(parts, flat, cube):
    count, rows, lanes = parts.shape
    rank = lanes // 2
    for owner in range(count):
        flat[owner * rows : (owner + 1) * rows, :] = parts[owner].astype(jnp.float32)
    half = rank // 2
    taps = count * rows // half
    whole = flat[...].reshape(taps, half, lanes)
    both = jnp.concatenate([whole[:, :, :rank], whole[:, :, rank:]], axis=1)
    cube[...] = both.reshape(taps * rank, rank).astype(jnp.bfloat16)


def step_kernel(
    grid_shape, cells_total,
    x_hbm, cot_hbm, core_hbm, one_hbm, two_hbm, uin_hbm, uout_hbm,
    fg_hbm, core_next_hbm, one_next_hbm, two_next_hbm, cube_hbm, pair_hbm,
    x_ref, cot_ref, core_ref, one_ref, two_ref, uin_ref, uout_ref,
    fg_ref, core_out, one_out, two_out, cube_out, pair_ref,
    wide_in, wide_out, taps_in, taps_out, flat, cube, parts, parts_next, send, recv,
    halo_send, halo_recv, all_send, all_recv, side_send, side_recv, load_sem, store_sem,
):
    n_rows, n_cols = grid_shape
    n = n_rows * n_cols
    my_row, my_col = lax.axis_index("rows"), lax.axis_index("cols")
    me = my_row * n_cols + my_col
    frames, rows, cols, chans = x_ref.shape
    cells = frames * rows * cols
    rank = uin_ref.shape[0]
    names = ("core", "u_in", "x", "u_out", "cot", "one", "two")
    pairs = (
        (core_hbm, core_ref), (uin_hbm, uin_ref), (x_hbm, x_ref), (uout_hbm, uout_ref),
        (cot_hbm, cot_ref), (one_hbm, one_ref), (two_hbm, two_ref),
    )
    loads = {
        name: pltpu.make_async_copy(source, target, load_sem.at[i])
        for i, (name, (source, target)) in enumerate(zip(names, pairs))
    }
    for load in loads.values():
        load.start()
    stores = [
        pltpu.make_async_copy(source, target, store_sem.at[i])
        for i, (source, target) in enumerate([
            (pair_ref, pair_hbm), (fg_ref, fg_hbm), (core_out, core_next_hbm),
            (one_out, one_next_hbm), (two_out, two_next_hbm), (cube_out, cube_hbm),
        ])
    ]

    def peer_of(k):
        peer = lax.rem(me + k, n)
        return peer, (lax.div(peer, n_cols), lax.rem(peer, n_cols))

    barrier = pltpu.get_barrier_semaphore()
    wide_in[...] = jnp.zeros_like(wide_in)
    wide_out[...] = jnp.zeros_like(wide_out)

    @pl.loop(1, n)
    def _(k):
        pl.semaphore_signal(barrier, inc=1, device_id=peer_of(k)[1], device_id_type=MESH)

    loads["core"].wait()
    parts[me] = core_ref[...].astype(jnp.bfloat16)
    loads["u_in"].wait()
    perm = pair_matrix(rank)
    u_in = dot(perm, uin_ref[...], ((1,), (0,))).astype(jnp.bfloat16)
    pair_ref[...] = dot(uin_ref[...], perm, ((0,), (1,))).astype(jnp.bfloat16)
    stores[0].start()
    loads["x"].wait()
    x = x_ref[...].astype(jnp.float32).reshape(cells, chans).astype(jnp.bfloat16)
    in_proj = dot(x, u_in, ((1,), (1,))).astype(jnp.bfloat16).astype(jnp.float32)
    wide_in[1, 1 : frames + 1, 1 : rows + 1] = in_proj.reshape(frames, rows, cols, rank)
    pl.semaphore_wait(barrier, n - 1)

    def halo_copy(wide, turn, slot):
        dr, dc = NEIGHBOURS[slot]
        inner = slice(1, rows + 1)
        source = {-1: slice(1, 2), 0: inner, 1: slice(rows, rows + 1)}[dr]
        edge = {-1: slice(0, 1), 0: slice(0, cols), 1: slice(cols - 1, cols)}[dc]
        target = {-1: slice(rows + 1, rows + 2), 0: inner, 1: slice(0, 1)}[dr]
        return pltpu.make_async_remote_copy(
            src_ref=wide.at[1, 1 : frames + 1, source, edge],
            dst_ref=wide.at[1 - dc, 1 : frames + 1, target, edge],
            send_sem=halo_send.at[turn, slot],
            recv_sem=halo_recv.at[turn, slot],
            device_id=(my_row + dr, my_col + dc),
            device_id_type=MESH,
        )

    def there(dr, dc):
        row, col = my_row + dr, my_col + dc
        return (row >= 0) & (row < n_rows) & (col >= 0) & (col < n_cols)

    def halo_each(wide, turn, act, sign):
        for slot, (dr, dc) in enumerate(NEIGHBOURS):
            if (dr != 0 and n_rows == 1) or (dc != 0 and n_cols == 1):
                continue

            @pl.when(there(sign * dr, sign * dc))
            def _():
                act(halo_copy(wide, turn, slot))

    def remote(source, target, sent, got, place):
        return pltpu.make_async_remote_copy(
            src_ref=source, dst_ref=target, send_sem=sent, recv_sem=got,
            device_id=place, device_id_type=MESH,
        )

    core = lax.rem(my_row, 2)
    chips = n // 2
    other = 1 - 2 * core
    sibling = (my_row + other, my_col)

    def chip_of(k):
        chip = lax.rem(lax.div(my_row, 2) * n_cols + my_col + k, chips)
        row, col = 2 * lax.div(chip, n_cols) + core, lax.rem(chip, n_cols)
        return row * n_cols + col, (row, col)

    def to_chip(turn, buffer, k):
        peer, place = chip_of(k)
        return remote(
            buffer.at[me], buffer.at[me], all_send.at[turn, peer], all_recv.at[turn, me], place
        )

    def to_sibling(turn, buffer, owner):
        return remote(
            buffer.at[owner], buffer.at[owner], side_send.at[turn, owner],
            side_recv.at[turn, owner], sibling,
        )

    def gather_start(turn, buffer):
        to_sibling(turn, buffer, me).start()

        @pl.loop(1, chips)
        def _(k):
            to_chip(turn, buffer, k).start()

    def gather_finish(turn, buffer):
        @pl.loop(1, chips)
        def _(k):
            owner, place = chip_of(k)
            remote(
                buffer.at[owner], buffer.at[owner], all_send.at[turn, owner],
                all_recv.at[turn, owner], place,
            ).wait_recv()
            to_sibling(turn, buffer, owner).start()

        @pl.loop(0, chips)
        def _(k):
            to_sibling(turn, buffer, chip_of(k)[0] + other * n_cols).wait_recv()

    def gather_sent(turn, buffer):
        @pl.loop(1, chips)
        def _(k):
            to_chip(turn, buffer, k).wait_send()

        @pl.loop(0, chips)
        def _(k):
            to_sibling(turn, buffer, chip_of(k)[0]).wait_send()

    def all_copy(turn, source, target, k):
        peer, place = peer_of(k)
        return remote(
            source(peer), target.at[me], all_send.at[turn, peer], all_recv.at[turn, me], place
        )

    def all_start(turn, source, target):
        @pl.loop(1, n, unroll=True)
        def _(k):
            all_copy(turn, source, target, k).start()

    def all_received(turn, target):
        @pl.loop(1, n, unroll=True)
        def _(k):
            peer, place = peer_of(k)
            remote(
                target.at[peer], target.at[peer], all_send.at[turn, peer],
                all_recv.at[turn, peer], place,
            ).wait_recv()

    def all_sent(turn, source, target):
        @pl.loop(1, n)
        def _(k):
            all_copy(turn, source, target, k).wait_send()

    halo_each(wide_in, 0, lambda copy: copy.start(), 1)
    gather_start(0, parts)
    halo_each(wide_in, 0, lambda copy: copy.wait_recv(), -1)
    fill_taps(wide_in, taps_in, False)
    gather_finish(0, parts)
    cube_rows(parts, flat, cube)

    mid = dot(taps_in[...], cube[...], ((1,), (0,))).astype(jnp.bfloat16)
    loads["u_out"].wait()
    u_out = uout_ref[...]
    pre = dot(mid, u_out, ((1,), (0,)))
    loads["cot"].wait()
    cot = cot_ref[...].astype(jnp.float32).reshape(cells, chans)
    sig = 1.0 / (1.0 + jnp.exp(-pre))
    slope = (cot * sig * (1.0 + pre * (1.0 - sig))).astype(jnp.bfloat16)
    out_proj = dot(slope, u_out, ((1,), (1,))).astype(jnp.bfloat16)
    wide_out[1, 1 : frames + 1, 1 : rows + 1] = out_proj.astype(jnp.float32).reshape(
        frames, rows, cols, rank
    )
    halo_each(wide_out, 1, lambda copy: copy.start(), 1)

    grad = dot(taps_in[...], out_proj, ((0,), (0,)))
    taps = grad.shape[0] // rank
    half = rank // 2
    grad = grad.reshape(taps, rank, rank)
    grad = jnp.concatenate([grad[:, :half], grad[:, half:]], axis=2)
    flat[...] = grad.reshape(taps * half, 2 * rank)
    part = core_ref.shape[0]
    for owner in range(n):
        send[owner] = flat[owner * part : (owner + 1) * part, :].astype(jnp.bfloat16)
    recv[me] = send[me]
    all_start(1, lambda peer: send.at[peer], recv)

    halo_each(wide_out, 1, lambda copy: copy.wait_recv(), -1)
    fill_taps(wide_out, taps_out, True)
    total = jnp.zeros((cells, rank), jnp.float32)
    for tap in range(taps):
        span = slice(rank * tap, rank * (tap + 1))
        total = total + dot(taps_out[:, span], cube[span, :], ((1,), (1,)))
    back = dot(total.astype(jnp.bfloat16), u_in, ((1,), (0,)))
    fg_ref[...] = back.reshape(frames, rows, cols, chans).astype(jnp.bfloat16)
    stores[1].start()

    halo_each(wide_in, 0, lambda copy: copy.wait_send(), 1)
    halo_each(wide_out, 1, lambda copy: copy.wait_send(), 1)
    gather_sent(0, parts)
    loads["one"].wait()
    loads["two"].wait()
    all_received(1, recv)
    summed = recv[0].astype(jnp.float32)
    for owner in range(1, n):
        summed = summed + recv[owner].astype(jnp.float32)
    core_grad = summed / math.sqrt(cells_total)
    one_next = beta_one * one_ref[...] + (1.0 - beta_one) * core_grad
    two_next = beta_two * two_ref[...] + (1.0 - beta_two) * core_grad * core_grad
    core_next = core_ref[...] - learn_rate * (one_next / fix_one) / (
        jnp.sqrt(two_next / fix_two) + epsilon
    )
    parts_next[me] = core_next.astype(jnp.bfloat16)
    all_start(2, lambda peer: parts_next.at[me], parts_next)
    core_out[...] = core_next
    one_out[...] = one_next
    two_out[...] = two_next
    for store in stores[2:5]:
        store.start()
    all_sent(1, lambda peer: send.at[peer], recv)
    all_received(2, parts_next)
    cube_rows(parts_next, flat, cube_out)
    stores[5].start()
    all_sent(2, lambda peer: parts_next.at[me], parts_next)
    for store in stores:
        store.wait()


def build_kernel(
    group, cube_hbm, uin_hbm, uout_hbm, fg_from, core_from, one_from, two_from,
    out_hbm, fg_to, core_to, one_to, two_to,
    cube_ref, uin_ref, uout_ref, fg_ref, core_ref, one_ref, two_ref, out_ref,
    in_sem, side_sem, out_sem,
):
    rank = uin_ref.shape[1]
    inner = (uout_ref, uin_ref, cube_ref, fg_ref, core_ref, one_ref, two_ref)
    outer = (uout_hbm, uin_hbm, cube_hbm, fg_from, core_from, one_from, two_from)
    final = (fg_to, core_to, one_to, two_to)
    loads = [
        pltpu.make_async_copy(source, target, in_sem.at[i])
        for i, (source, target) in enumerate(zip(outer, inner))
    ]
    sides = [
        pltpu.make_async_copy(source, target, side_sem.at[i])
        for i, (source, target) in enumerate(zip(inner[3:], final))
    ]
    for load in loads:
        load.start()
    for load in loads[:3]:
        load.wait()
    u_in = uin_ref[...]
    u_out = uout_ref[...]
    copies = []
    for first in range(0, out_ref.shape[0], group):
        cube = cube_ref[rank * first : rank * (first + group), :]
        halfway = dot(cube, u_out, ((1,), (0,))).astype(jnp.bfloat16)
        for tap in range(group):
            span = slice(rank * tap, rank * (tap + 1))
            out_ref[first + tap] = dot(u_in, halfway[span], ((1,), (0,))).astype(jnp.bfloat16)
        block = pl.ds(first, group)
        copy = pltpu.make_async_copy(
            out_ref.at[block], out_hbm.at[block], out_sem.at[first // group]
        )
        copy.start()
        copies.append(copy)
        if first == 0:
            for load, side in zip(loads[3:], sides):
                load.wait()
                side.start()
    for copy in sides + copies:
        copy.wait()


def fused_body(frames_in, cotangent, core, moment_one, moment_two, u_in, u_out):
    frames, rows, cols, chans = frames_in.shape
    rank = u_in.shape[1]
    grid_shape = (lax.axis_size("rows"), lax.axis_size("cols"))
    n = grid_shape[0] * grid_shape[1]
    lanes = 2 * rank
    part = core.shape[0] // lanes
    taps = n * core.shape[0] // (rank * rank)
    cells = frames * rows * cols
    f32, bf16 = jnp.float32, jnp.bfloat16
    hbm = pl.BlockSpec(memory_space=pltpu.HBM)
    upright = jax.ShapeDtypeStruct((chans, rank), bf16)
    block = pltpu.VMEM(frames_in.shape, bf16)
    flat_vmem = pltpu.VMEM((part, lanes), f32)
    factor = pltpu.VMEM((rank, chans), bf16)
    cube_vmem = pltpu.VMEM((taps * rank, rank), bf16)
    flat_shape = jax.ShapeDtypeStruct((part, lanes), f32)
    wide = pltpu.VMEM((3, frames + 2, rows + 2, cols, rank), f32)
    pieces = pltpu.VMEM((n, part, lanes), bf16)
    *sides, cube_next, uin_next = pl.pallas_call(
        functools.partial(step_kernel, grid_shape, cells * n),
        out_shape=(
            jax.ShapeDtypeStruct(frames_in.shape, bf16),
            flat_shape,
            flat_shape,
            flat_shape,
            jax.ShapeDtypeStruct((taps * rank, rank), bf16),
            upright,
        ),
        in_specs=[hbm] * 7,
        out_specs=[hbm] * 6,
        scratch_shapes=[
            block,
            block,
            flat_vmem,
            flat_vmem,
            flat_vmem,
            factor,
            factor,
            block,
            flat_vmem,
            flat_vmem,
            flat_vmem,
            cube_vmem,
            pltpu.VMEM((chans, rank), bf16),
            wide,
            wide,
            pltpu.VMEM((cells, taps * rank), bf16),
            pltpu.VMEM((cells, taps * rank), bf16),
            pltpu.VMEM((n * part, lanes), f32),
            pltpu.VMEM((taps * rank, rank), bf16),
            pieces,
            pieces,
            pieces,
            pieces,
            pltpu.SemaphoreType.DMA((2, 8)),
            pltpu.SemaphoreType.DMA((2, 8)),
            pltpu.SemaphoreType.DMA((3, n)),
            pltpu.SemaphoreType.DMA((3, n)),
            pltpu.SemaphoreType.DMA((3, n)),
            pltpu.SemaphoreType.DMA((3, n)),
            pltpu.SemaphoreType.DMA((7,)),
            pltpu.SemaphoreType.DMA((6,)),
        ],
        compiler_params=pltpu.CompilerParams(
            collective_id=0, has_side_effects=True, vmem_limit_bytes=vmem_limit
        ),
        name="step",
    )(
        frames_in,
        cotangent,
        core.reshape(part, lanes),
        moment_one.reshape(part, lanes),
        moment_two.reshape(part, lanes),
        u_in.T,
        u_out.T,
    )
    group = 9 if taps % 9 == 0 else 1
    kernel_next, fg, core_next, one_next, two_next = pl.pallas_call(
        functools.partial(build_kernel, group),
        out_shape=(
            jax.ShapeDtypeStruct((taps, chans, chans), bf16),
            jax.ShapeDtypeStruct(frames_in.shape, bf16),
            flat_shape,
            flat_shape,
            flat_shape,
        ),
        in_specs=[hbm] * 7,
        out_specs=[hbm] * 5,
        scratch_shapes=[
            cube_vmem,
            pltpu.VMEM((chans, rank), bf16),
            factor,
            block,
            flat_vmem,
            flat_vmem,
            flat_vmem,
            pltpu.VMEM((taps, chans, chans), bf16),
            pltpu.SemaphoreType.DMA((7,)),
            pltpu.SemaphoreType.DMA((4,)),
            pltpu.SemaphoreType.DMA((taps // group,)),
        ],
        compiler_params=pltpu.CompilerParams(vmem_limit_bytes=vmem_limit),
        name="build",
    )(cube_next, uin_next, u_out.T, *sides)
    return (
        fg,
        core_next.reshape(-1),
        one_next.reshape(-1),
        two_next.reshape(-1),
        kernel_next,
    )


def body(frames_in, cotangent, core, moment_one, moment_two, u_in, u_out):
    lanes = 2 * u_in.shape[1]
    aligned = lanes == 128 and core.shape[0] % lanes == 0 and frames_in.shape[2] == 8
    if aligned and lax.axis_size("rows") % 2 == 0:
        step = fused_body
    else:
        step = plain_body
    return step(frames_in, cotangent, core, moment_one, moment_two, u_in, u_out)


def solution(mesh):
    in_specs = (
        P(None, "rows", "cols", None),
        P(None, "rows", "cols", None),
        P(("rows", "cols")),
        P(("rows", "cols")),
        P(("rows", "cols")),
        P(),
        P(),
    )
    out_specs = (
        P(None, "rows", "cols", None),
        P(("rows", "cols")),
        P(("rows", "cols")),
        P(("rows", "cols")),
        P(),
    )
    return jax.shard_map(body, mesh=mesh, in_specs=in_specs, out_specs=out_specs, check_vma=False)
```

profile of v0, /device:TPU:9, one launch (start us, length us, event | category | flops | bytes accessed | tf_op | source)
XLA Modules:
  0.0 37.4 jit_solution(10686437874829183044)
XLA Ops:
  0.6 32.8 %step.1 = (bf16[3,6,8,256]{3,2,1,0:T(8,128)(2,1)}, f32[27,128]{1,0:T(8,128)}, f32[27,128]{1,0:T(8,128)}, f32[27,128]{1,0:T(8,128)}, bf16[1728,64]{1,0:T(8,128)(2,1)}, /*index=5*/bf16[256,64]{1,0:T(8,128)(2,1)}) custom-call(bf16[3,6,8,256]{3,2,1,0:T(8,128)(2,1)} %x_hbm.1, bf16[3,6,8,256]{3,2,1,0:T(8,128)(2,1)} %cot_hbm.1, f32[27,128]{1,0:T(8,128)} %bitcast.11, ...), custom_call_target="tpu_custom_call" | custom-call | tf_op jit(solution)/shard_map/step/pallas_call | solution.py:496
  33.4 3.9 %build.1 = (bf16[27,256,256]{2,1,0:T(8,128)(2,1)}, bf16[3,6,8,256]{3,2,1,0:T(8,128)(2,1)}, f32[27,128]{1,0:T(8,128)}, f32[27,128]{1,0:T(8,128)}, f32[27,128]{1,0:T(8,128)}) custom-call(bf16[1728,64]{1,0:T(8,128)(2,1)} %get-tuple-element.16.cube_hbm, bf16[256,64]{1,0:T(8,128)(2,1)} %get-tuple-element.17.uin_hbm, bf16[64,256]{1,0:T(8,128)(2,1)} %bitcast.9, ...), custom_call_target="tpu_custom_call" | custom-call | tf_op jit(solution)/shard_map/build/pallas_call | solution.py:555
where the time goes:
time: 37.6 us; the launch traced here: 37.4 us
  Pallas kernels  36.7 us (98%)
  between operations  0.64 us (2%)
    pallas_call x1, Pallas kernels, fused_body(): pl.pallas_call(functools.partial(step_kernel, grid_shape, cells * n), out...  32.8 us
    pallas_call x1, Pallas kernels, fused_body(): pl.pallas_call(functools.partial(build_kernel, group), out_shape=(jax.Sha...  3.93 us

commit v1 on v0

--- a/solution.py
+++ b/solution.py
@@ -125,7 +125,7 @@
 
 
 MESH = pl.DeviceIdType.MESH
-vmem_limit = 67043328
+vmem_limit = 33554432
 NEIGHBOURS = [(dr, dc) for dr in (-1, 0, 1) for dc in (-1, 0, 1) if (dr, dc) != (0, 0)]
 
 
@@ -172,11 +172,18 @@
         out[:, rank * tap : rank * (tap + 1)] = piece.astype(jnp.bfloat16)
 
 
-def cube_rows(parts, flat, cube):
-    count, rows, lanes = parts.shape
+def seat(owner, n_cols):
+    row, col = owner // n_cols, owner % n_cols
+    return row % 2, row // 2 * n_cols + col
+
+
+def cube_rows(parts, grid_shape, flat, cube):
+    _, _, rows, lanes = parts.shape
+    count = grid_shape[0] * grid_shape[1]
     rank = lanes // 2
     for owner in range(count):
-        flat[owner * rows : (owner + 1) * rows, :] = parts[owner].astype(jnp.float32)
+        piece = parts[seat(owner, grid_shape[1])]
+        flat[owner * rows : (owner + 1) * rows, :] = piece.astype(jnp.float32)
     half = rank // 2
     taps = count * rows // half
     whole = flat[...].reshape(taps, half, lanes)
@@ -184,19 +191,32 @@
     cube[...] = both.reshape(taps * rank, rank).astype(jnp.bfloat16)
 
 
+def flipped(index, mask):
+    result, bit = index, 1
+    while bit <= mask:
+        if mask & bit:
+            result = result + bit * (1 - 2 * lax.rem(lax.div(index, bit), 2))
+        bit *= 2
+    return result
+
+
 def step_kernel(
     grid_shape, cells_total,
     x_hbm, cot_hbm, core_hbm, one_hbm, two_hbm, uin_hbm, uout_hbm,
-    fg_hbm, core_next_hbm, one_next_hbm, two_next_hbm, cube_hbm, pair_hbm,
-    x_ref, cot_ref, core_ref, one_ref, two_ref, uin_ref, uout_ref,
-    fg_ref, core_out, one_out, two_out, cube_out, pair_ref,
-    wide_in, wide_out, taps_in, taps_out, flat, cube, parts, parts_next, send, recv,
-    halo_send, halo_recv, all_send, all_recv, side_send, side_recv, load_sem, store_sem,
+    fg_ref, core_out, one_out, two_out, cube_out, pair_ref, uout_ref,
+    x_ref, cot_ref, core_ref, one_ref, two_ref, uin_ref,
+    wide_in, wide_out, taps_in, taps_out, flat, cube, parts, parts_next,
+    mine, theirs, send, recv,
+    halo_send, halo_recv, chip_send, chip_recv, sum_recv, side_send, side_recv, load_sem,
 ):
     n_rows, n_cols = grid_shape
     n = n_rows * n_cols
+    chips = n // 2
     my_row, my_col = lax.axis_index("rows"), lax.axis_index("cols")
-    me = my_row * n_cols + my_col
+    core = lax.rem(my_row, 2)
+    other = 1 - core
+    chip = lax.div(my_row, 2) * n_cols + my_col
+    sibling = (my_row + other - core, my_col)
     frames, rows, cols, chans = x_ref.shape
     cells = frames * rows * cols
     rank = uin_ref.shape[0]
@@ -211,38 +231,78 @@
     }
     for load in loads.values():
         load.start()
-    stores = [
-        pltpu.make_async_copy(source, target, store_sem.at[i])
-        for i, (source, target) in enumerate([
-            (pair_ref, pair_hbm), (fg_ref, fg_hbm), (core_out, core_next_hbm),
-            (one_out, one_next_hbm), (two_out, two_next_hbm), (cube_out, cube_hbm),
-        ])
-    ]
-
-    def peer_of(k):
-        peer = lax.rem(me + k, n)
-        return peer, (lax.div(peer, n_cols), lax.rem(peer, n_cols))
-
+
+    def place(mask, on_core):
+        peer = flipped(chip, mask)
+        return (2 * lax.div(peer, n_cols) + on_core, lax.rem(peer, n_cols))
+
+    wide_in[...] = jnp.zeros_like(wide_in)
     barrier = pltpu.get_barrier_semaphore()
-    wide_in[...] = jnp.zeros_like(wide_in)
+    for mask in range(chips - 1, -1, -1):
+        for on_core in (core, other) if mask else (other,):
+            pl.semaphore_signal(
+                barrier, inc=1, device_id=place(mask, on_core), device_id_type=MESH
+            )
     wide_out[...] = jnp.zeros_like(wide_out)
 
-    @pl.loop(1, n)
-    def _(k):
-        pl.semaphore_signal(barrier, inc=1, device_id=peer_of(k)[1], device_id_type=MESH)
+    def remote(source, target, sent, got, where):
+        return pltpu.make_async_remote_copy(
+            src_ref=source, dst_ref=target, send_sem=sent, recv_sem=got,
+            device_id=where, device_id_type=MESH,
+        )
+
+    def to_chip(turn, buffer, mask):
+        piece = buffer.at[core, chip]
+        return remote(piece, piece, chip_send.at[turn], chip_recv.at[mask - 1], place(mask, core))
+
+    def to_far_side(turn, buffer, mask):
+        piece = buffer.at[core, chip]
+        return remote(piece, piece, side_send.at[turn], side_recv.at[turn], place(mask, other))
+
+    def to_sibling(turn, buffer, mask):
+        piece = buffer.at[core, flipped(chip, mask)]
+        return remote(piece, piece, side_send.at[turn], side_recv.at[turn], sibling)
+
+    direct = ()
+
+    def gather_start(turn, buffer):
+        for mask in range(chips - 1, 0, -1):
+            to_chip(turn, buffer, mask).start()
+            if mask in direct:
+                to_far_side(turn, buffer, mask).start()
+        to_sibling(turn, buffer, 0).start()
+
+    def gather_finish(turn, buffer):
+        for mask in range(1, chips):
+            piece = buffer.at[core, flipped(chip, mask)]
+            remote(
+                piece, piece, chip_send.at[turn], chip_recv.at[mask - 1], place(mask, core)
+            ).wait_recv()
+            if mask not in direct:
+                to_sibling(turn, buffer, mask).start()
+        remote(
+            buffer.at[other], buffer.at[other], side_send.at[turn], side_recv.at[turn], sibling
+        ).wait_recv()
+
+    def gather_sent(turn, buffer):
+        some = buffer.at[0, pl.ds(0, chips - 1)]
+        remote(some, some, chip_send.at[turn], chip_recv.at[0], sibling).wait_send()
+        remote(
+            buffer.at[0], buffer.at[0], side_send.at[turn], side_recv.at[turn], sibling
+        ).wait_send()
 
     loads["core"].wait()
-    parts[me] = core_ref[...].astype(jnp.bfloat16)
+    parts[core, chip] = core_ref[...].astype(jnp.bfloat16)
+    pl.semaphore_wait(barrier, n - 1)
+    gather_start(0, parts)
     loads["u_in"].wait()
     perm = pair_matrix(rank)
     u_in = dot(perm, uin_ref[...], ((1,), (0,))).astype(jnp.bfloat16)
     pair_ref[...] = dot(uin_ref[...], perm, ((0,), (1,))).astype(jnp.bfloat16)
-    stores[0].start()
     loads["x"].wait()
     x = x_ref[...].astype(jnp.float32).reshape(cells, chans).astype(jnp.bfloat16)
     in_proj = dot(x, u_in, ((1,), (1,))).astype(jnp.bfloat16).astype(jnp.float32)
     wide_in[1, 1 : frames + 1, 1 : rows + 1] = in_proj.reshape(frames, rows, cols, rank)
-    pl.semaphore_wait(barrier, n - 1)
 
     def halo_copy(wide, turn, slot):
         dr, dc = NEIGHBOURS[slot]
@@ -250,11 +310,12 @@
         source = {-1: slice(1, 2), 0: inner, 1: slice(rows, rows + 1)}[dr]
         edge = {-1: slice(0, 1), 0: slice(0, cols), 1: slice(cols - 1, cols)}[dc]
         target = {-1: slice(rows + 1, rows + 2), 0: inner, 1: slice(0, 1)}[dr]
+        side = 0 if dc == 0 else 1 if n_cols == 2 else 1 + (dc + 1) // 2
         return pltpu.make_async_remote_copy(
             src_ref=wide.at[1, 1 : frames + 1, source, edge],
             dst_ref=wide.at[1 - dc, 1 : frames + 1, target, edge],
-            send_sem=halo_send.at[turn, slot],
-            recv_sem=halo_recv.at[turn, slot],
+            send_sem=halo_send.at[turn, dr + 1, side],
+            recv_sem=halo_recv.at[turn, dr + 1, side],
             device_id=(my_row + dr, my_col + dc),
             device_id_type=MESH,
         )
@@ -272,95 +333,11 @@
             def _():
                 act(halo_copy(wide, turn, slot))
 
-    def remote(source, target, sent, got, place):
-        return pltpu.make_async_remote_copy(
-            src_ref=source, dst_ref=target, send_sem=sent, recv_sem=got,
-            device_id=place, device_id_type=MESH,
-        )
-
-    core = lax.rem(my_row, 2)
-    chips = n // 2
-    other = 1 - 2 * core
-    sibling = (my_row + other, my_col)
-
-    def chip_of(k):
-        chip = lax.rem(lax.div(my_row, 2) * n_cols + my_col + k, chips)
-        row, col = 2 * lax.div(chip, n_cols) + core, lax.rem(chip, n_cols)
-        return row * n_cols + col, (row, col)
-
-    def to_chip(turn, buffer, k):
-        peer, place = chip_of(k)
-        return remote(
-            buffer.at[me], buffer.at[me], all_send.at[turn, peer], all_recv.at[turn, me], place
-        )
-
-    def to_sibling(turn, buffer, owner):
-        return remote(
-            buffer.at[owner], buffer.at[owner], side_send.at[turn, owner],
-            side_recv.at[turn, owner], sibling,
-        )
-
-    def gather_start(turn, buffer):
-        to_sibling(turn, buffer, me).start()
-
-        @pl.loop(1, chips)
-        def _(k):
-            to_chip(turn, buffer, k).start()
-
-    def gather_finish(turn, buffer):
-        @pl.loop(1, chips)
-        def _(k):
-            owner, place = chip_of(k)
-            remote(
-                buffer.at[owner], buffer.at[owner], all_send.at[turn, owner],
-                all_recv.at[turn, owner], place,
-            ).wait_recv()
-            to_sibling(turn, buffer, owner).start()
-
-        @pl.loop(0, chips)
-        def _(k):
-            to_sibling(turn, buffer, chip_of(k)[0] + other * n_cols).wait_recv()
-
-    def gather_sent(turn, buffer):
-        @pl.loop(1, chips)
-        def _(k):
-            to_chip(turn, buffer, k).wait_send()
-
-        @pl.loop(0, chips)
-        def _(k):
-            to_sibling(turn, buffer, chip_of(k)[0]).wait_send()
-
-    def all_copy(turn, source, target, k):
-        peer, place = peer_of(k)
-        return remote(
-            source(peer), target.at[me], all_send.at[turn, peer], all_recv.at[turn, me], place
-        )
-
-    def all_start(turn, source, target):
-        @pl.loop(1, n, unroll=True)
-        def _(k):
-            all_copy(turn, source, target, k).start()
-
-    def all_received(turn, target):
-        @pl.loop(1, n, unroll=True)
-        def _(k):
-            peer, place = peer_of(k)
-            remote(
-                target.at[peer], target.at[peer], all_send.at[turn, peer],
-                all_recv.at[turn, peer], place,
-            ).wait_recv()
-
-    def all_sent(turn, source, target):
-        @pl.loop(1, n)
-        def _(k):
-            all_copy(turn, source, target, k).wait_send()
-
     halo_each(wide_in, 0, lambda copy: copy.start(), 1)
-    gather_start(0, parts)
     halo_each(wide_in, 0, lambda copy: copy.wait_recv(), -1)
     fill_taps(wide_in, taps_in, False)
     gather_finish(0, parts)
-    cube_rows(parts, flat, cube)
+    cube_rows(parts, grid_shape, flat, cube)
 
     mid = dot(taps_in[...], cube[...], ((1,), (0,))).astype(jnp.bfloat16)
     loads["u_out"].wait()
@@ -384,9 +361,25 @@
     flat[...] = grad.reshape(taps * half, 2 * rank)
     part = core_ref.shape[0]
     for owner in range(n):
-        send[owner] = flat[owner * part : (owner + 1) * part, :].astype(jnp.bfloat16)
-    recv[me] = send[me]
-    all_start(1, lambda peer: send.at[peer], recv)
+        on_core, on_chip = seat(owner, n_cols)
+        mine[on_core, on_chip] = flat[owner * part : (owner + 1) * part, :].astype(jnp.bfloat16)
+    pair_up = remote(mine.at[other], theirs, side_send.at[1], side_recv.at[1], sibling)
+    pair_up.start()
+    pair_up.wait_recv()
+    for k in range(chips):
+        send[k] = (mine[core, k].astype(jnp.float32) + theirs[k].astype(jnp.float32)).astype(
+            jnp.bfloat16
+        )
+
+    def share(mask):
+        return remote(
+            send.at[flipped(chip, mask)], recv.at[chip], chip_send.at[1], sum_recv.at[0],
+            place(mask, core),
+        )
+
+    for mask in range(chips - 1, 0, -1):
+        share(mask).start()
+    recv[chip] = send[chip]
 
     halo_each(wide_out, 1, lambda copy: copy.wait_recv(), -1)
     fill_taps(wide_out, taps_out, True)
@@ -396,61 +389,47 @@
         total = total + dot(taps_out[:, span], cube[span, :], ((1,), (1,)))
     back = dot(total.astype(jnp.bfloat16), u_in, ((1,), (0,)))
     fg_ref[...] = back.reshape(frames, rows, cols, chans).astype(jnp.bfloat16)
-    stores[1].start()
 
     halo_each(wide_in, 0, lambda copy: copy.wait_send(), 1)
     halo_each(wide_out, 1, lambda copy: copy.wait_send(), 1)
     gather_sent(0, parts)
+    pair_up.wait_send()
     loads["one"].wait()
     loads["two"].wait()
-    all_received(1, recv)
+    some = recv.at[pl.ds(0, chips - 1)]
+    shares = remote(some, some, chip_send.at[1], sum_recv.at[0], sibling)
+    shares.wait_recv()
     summed = recv[0].astype(jnp.float32)
-    for owner in range(1, n):
-        summed = summed + recv[owner].astype(jnp.float32)
+    for k in range(1, chips):
+        summed = summed + recv[k].astype(jnp.float32)
     core_grad = summed / math.sqrt(cells_total)
     one_next = beta_one * one_ref[...] + (1.0 - beta_one) * core_grad
     two_next = beta_two * two_ref[...] + (1.0 - beta_two) * core_grad * core_grad
     core_next = core_ref[...] - learn_rate * (one_next / fix_one) / (
         jnp.sqrt(two_next / fix_two) + epsilon
     )
-    parts_next[me] = core_next.astype(jnp.bfloat16)
-    all_start(2, lambda peer: parts_next.at[me], parts_next)
+    parts_next[core, chip] = core_next.astype(jnp.bfloat16)
+    gather_start(2, parts_next)
     core_out[...] = core_next
     one_out[...] = one_next
     two_out[...] = two_next
-    for store in stores[2:5]:
-        store.start()
-    all_sent(1, lambda peer: send.at[peer], recv)
-    all_received(2, parts_next)
-    cube_rows(parts_next, flat, cube_out)
-    stores[5].start()
-    all_sent(2, lambda peer: parts_next.at[me], parts_next)
-    for store in stores:
-        store.wait()
+    shares.wait_send()
+    gather_finish(2, parts_next)
+    cube_rows(parts_next, grid_shape, flat, cube_out)
+    gather_sent(2, parts_next)
 
 
 def build_kernel(
-    group, cube_hbm, uin_hbm, uout_hbm, fg_from, core_from, one_from, two_from,
-    out_hbm, fg_to, core_to, one_to, two_to,
-    cube_ref, uin_ref, uout_ref, fg_ref, core_ref, one_ref, two_ref, out_ref,
-    in_sem, side_sem, out_sem,
+    group, cube_ref, uin_ref, uout_ref, fg_from, core_from, one_from, two_from,
+    out_hbm, fg_to, core_to, one_to, two_to, out_ref, side_sem, out_sem,
 ):
     rank = uin_ref.shape[1]
-    inner = (uout_ref, uin_ref, cube_ref, fg_ref, core_ref, one_ref, two_ref)
-    outer = (uout_hbm, uin_hbm, cube_hbm, fg_from, core_from, one_from, two_from)
+    inner = (fg_from, core_from, one_from, two_from)
     final = (fg_to, core_to, one_to, two_to)
-    loads = [
-        pltpu.make_async_copy(source, target, in_sem.at[i])
-        for i, (source, target) in enumerate(zip(outer, inner))
-    ]
     sides = [
         pltpu.make_async_copy(source, target, side_sem.at[i])
-        for i, (source, target) in enumerate(zip(inner[3:], final))
+        for i, (source, target) in enumerate(zip(inner, final))
     ]
-    for load in loads:
-        load.start()
-    for load in loads[:3]:
-        load.wait()
     u_in = uin_ref[...]
     u_out = uout_ref[...]
     copies = []
@@ -467,8 +446,7 @@
         copy.start()
         copies.append(copy)
         if first == 0:
-            for load, side in zip(loads[3:], sides):
-                load.wait()
+            for side in sides:
                 side.start()
     for copy in sides + copies:
         copy.wait()
@@ -479,32 +457,38 @@
     rank = u_in.shape[1]
     grid_shape = (lax.axis_size("rows"), lax.axis_size("cols"))
     n = grid_shape[0] * grid_shape[1]
+    chips = n // 2
     lanes = 2 * rank
     part = core.shape[0] // lanes
     taps = n * core.shape[0] // (rank * rank)
     cells = frames * rows * cols
+    sides_of = 2 if grid_shape[1] == 2 else 3
     f32, bf16 = jnp.float32, jnp.bfloat16
     hbm = pl.BlockSpec(memory_space=pltpu.HBM)
-    upright = jax.ShapeDtypeStruct((chans, rank), bf16)
+    vmem = pl.BlockSpec(memory_space=pltpu.VMEM)
     block = pltpu.VMEM(frames_in.shape, bf16)
     flat_vmem = pltpu.VMEM((part, lanes), f32)
     factor = pltpu.VMEM((rank, chans), bf16)
     cube_vmem = pltpu.VMEM((taps * rank, rank), bf16)
     flat_shape = jax.ShapeDtypeStruct((part, lanes), f32)
     wide = pltpu.VMEM((3, frames + 2, rows + 2, cols, rank), f32)
-    pieces = pltpu.VMEM((n, part, lanes), bf16)
-    *sides, cube_next, uin_next = pl.pallas_call(
+    pieces = pltpu.VMEM((2, chips, part, lanes), bf16)
+    sums = pltpu.VMEM((chips, part, lanes), bf16)
+    in_hbm = functools.partial(pltpu.with_memory_space_constraint, memory_space=pltpu.HBM)
+    in_vmem = functools.partial(pltpu.with_memory_space_constraint, memory_space=pltpu.VMEM)
+    *sides, cube_next, uin_next, uout_next = pl.pallas_call(
         functools.partial(step_kernel, grid_shape, cells * n),
         out_shape=(
-            jax.ShapeDtypeStruct(frames_in.shape, bf16),
-            flat_shape,
-            flat_shape,
-            flat_shape,
-            jax.ShapeDtypeStruct((taps * rank, rank), bf16),
-            upright,
+            block,
+            flat_vmem,
+            flat_vmem,
+            flat_vmem,
+            cube_vmem,
+            pltpu.VMEM((chans, rank), bf16),
+            factor,
         ),
         in_specs=[hbm] * 7,
-        out_specs=[hbm] * 6,
+        out_specs=[vmem] * 7,
         scratch_shapes=[
             block,
             block,
@@ -512,13 +496,6 @@
             flat_vmem,
             flat_vmem,
             factor,
-            factor,
-            block,
-            flat_vmem,
-            flat_vmem,
-            flat_vmem,
-            cube_vmem,
-            pltpu.VMEM((chans, rank), bf16),
             wide,
             wide,
             pltpu.VMEM((cells, taps * rank), bf16),
@@ -528,28 +505,30 @@
             pieces,
             pieces,
             pieces,
-            pieces,
-            pltpu.SemaphoreType.DMA((2, 8)),
-            pltpu.SemaphoreType.DMA((2, 8)),
-            pltpu.SemaphoreType.DMA((3, n)),
-            pltpu.SemaphoreType.DMA((3, n)),
-            pltpu.SemaphoreType.DMA((3, n)),
-            pltpu.SemaphoreType.DMA((3, n)),
+            sums,
+            sums,
+            sums,
+            pltpu.SemaphoreType.DMA((2, 3, sides_of)),
+            pltpu.SemaphoreType.DMA((2, 3, sides_of)),
+            pltpu.SemaphoreType.DMA((3,)),
+            pltpu.SemaphoreType.DMA((chips - 1,)),
+            pltpu.SemaphoreType.DMA((1,)),
+            pltpu.SemaphoreType.DMA((3,)),
+            pltpu.SemaphoreType.DMA((3,)),
             pltpu.SemaphoreType.DMA((7,)),
-            pltpu.SemaphoreType.DMA((6,)),
         ],
         compiler_params=pltpu.CompilerParams(
             collective_id=0, has_side_effects=True, vmem_limit_bytes=vmem_limit
         ),
         name="step",
     )(
-        frames_in,
-        cotangent,
-        core.reshape(part, lanes),
-        moment_one.reshape(part, lanes),
-        moment_two.reshape(part, lanes),
-        u_in.T,
-        u_out.T,
+        in_hbm(frames_in),
+        in_hbm(cotangent),
+        in_hbm(core.reshape(part, lanes)),
+        in_hbm(moment_one.reshape(part, lanes)),
+        in_hbm(moment_two.reshape(part, lanes)),
+        in_hbm(u_in.T),
+        in_hbm(u_out.T),
     )
     group = 9 if taps % 9 == 0 else 1
     kernel_next, fg, core_next, one_next, two_next = pl.pallas_call(
@@ -561,24 +540,16 @@
             flat_shape,
             flat_shape,
         ),
-        in_specs=[hbm] * 7,
+        in_specs=[vmem] * 7,
         out_specs=[hbm] * 5,
         scratch_shapes=[
-            cube_vmem,
-            pltpu.VMEM((chans, rank), bf16),
-            factor,
-            block,
-            flat_vmem,
-            flat_vmem,
-            flat_vmem,
             pltpu.VMEM((taps, chans, chans), bf16),
-            pltpu.SemaphoreType.DMA((7,)),
             pltpu.SemaphoreType.DMA((4,)),
             pltpu.SemaphoreType.DMA((taps // group,)),
         ],
         compiler_params=pltpu.CompilerParams(vmem_limit_bytes=vmem_limit),
         name="build",
-    )(cube_next, uin_next, u_out.T, *sides)
+    )(*(in_vmem(array) for array in (cube_next, uin_next, uout_next, *sides)))
     return (
         fg,
         core_next.reshape(-1),
@@ -591,7 +562,8 @@
 def body(frames_in, cotangent, core, moment_one, moment_two, u_in, u_out):
     lanes = 2 * u_in.shape[1]
     aligned = lanes == 128 and core.shape[0] % lanes == 0 and frames_in.shape[2] == 8
-    if aligned and lax.axis_size("rows") % 2 == 0:
+    chips = lax.axis_size("rows") * lax.axis_size("cols") // 2
+    if aligned and lax.axis_size("rows") % 2 == 0 and chips & (chips - 1) == 0:
         step = fused_body
     else:
         step = plain_body

time: 37.6 us -> 30.5 us (0.81)
  the two profiles are of different devices: /device:TPU:9 before, /device:TPU:0 now
where the time goes in v1:
time: 30.5 us; the launch traced here: 30.2 us
  Pallas kernels  29.6 us (97%)
  between operations  0.64 us (2%)
    pallas_call x1, Pallas kernels, fused_body(): pl.pallas_call(functools.partial(step_kernel, grid_shape, cells * n), out...  27.1 us
    pallas_call x1, Pallas kernels, fused_body(): pl.pallas_call(functools.partial(build_kernel, group), out_shape=(jax.Sha...  2.54 us

profile of v1, /device:TPU:0, one launch (start us, length us, event | category | flops | bytes accessed | tf_op | source)
XLA Modules:
  0.0 30.2 jit_solution(10881566531897251873)
XLA Ops:
  0.6 27.1 %step.1 = (bf16[3,6,8,256]{3,2,1,0:T(8,128)(2,1)S(1)}, f32[27,128]{1,0:T(8,128)S(1)}, f32[27,128]{1,0:T(8,128)S(1)}, f32[27,128]{1,0:T(8,128)S(1)}, bf16[1728,64...) custom-call(bf16[3,6,8,256]{3,2,1,0:T(8,128)(2,1)} %x_hbm.1, ...), custom_call_target="tpu_custom_call" | custom-call | tf_op jit(solution)/shard_map/step/pallas_call | solution.py:479
  27.7 2.5 %build.1 = (bf16[27,256,256]{2,1,0:T(8,128)(2,1)}, bf16[3,6,8,256]{3,2,1,0:T(8,128)(2,1)}, f32[27,128]{1,0:T(8,128)}, f32[27,128]{1,0:T(8,128)}, f32[27,128]{1,0:T(8,128)}) custom-call(bf16[1728,64]{1,0:T(8,128)(2,1)S(1)} %get-tuple-element.17.cube_ref, bf16[256,64]{1,0:T(8,128)(2,1)S(1)} %get-tuple-element.18.uin_ref, ...), custom_call_target="tpu_custom_call" | custom-call | tf_op jit(solution)/shard_map/build/pallas_call | solution.py:534

commit v2 on v1

--- a/solution.py
+++ b/solution.py
@@ -207,7 +207,7 @@
     x_ref, cot_ref, core_ref, one_ref, two_ref, uin_ref,
     wide_in, wide_out, taps_in, taps_out, flat, cube, parts, parts_next,
     mine, theirs, send, recv,
-    halo_send, halo_recv, chip_send, chip_recv, sum_recv, side_send, side_recv, load_sem,
+    halo_send, halo_recv, chip_send, plane_recv, sum_recv, side_send, side_recv, load_sem,
 ):
     n_rows, n_cols = grid_shape
     n = n_rows * n_cols
@@ -232,16 +232,19 @@
     for load in loads.values():
         load.start()
 
-    def place(mask, on_core):
-        peer = flipped(chip, mask)
+    def seat_of(peer, on_core):
         return (2 * lax.div(peer, n_cols) + on_core, lax.rem(peer, n_cols))
 
     wide_in[...] = jnp.zeros_like(wide_in)
+    near = min(4, chips)
+    planes = chips // near
+    plane = lax.div(chip, near)
     barrier = pltpu.get_barrier_semaphore()
     for mask in range(chips - 1, -1, -1):
         for on_core in (core, other) if mask else (other,):
             pl.semaphore_signal(
-                barrier, inc=1, device_id=place(mask, on_core), device_id_type=MESH
+                barrier, inc=1, device_id=seat_of(flipped(chip, mask), on_core),
+                device_id_type=MESH,
             )
     wide_out[...] = jnp.zeros_like(wide_out)
 
@@ -251,59 +254,48 @@
             device_id=where, device_id_type=MESH,
         )
 
-    def to_chip(turn, buffer, mask):
+    def shift_of(peer):
+        return lax.rem(plane - lax.div(peer, near) + planes, planes)
+
+    def to_sibling(turn, buffer, step):
+        group = buffer.at[core, pl.ds(near * lax.rem(plane + step, planes), near)]
+        return remote(group, group, side_send.at[turn], side_recv.at[turn], sibling)
+
+    def each_peer(turn, act):
+        for i in range(chips - 1) if turn != 1 else range(chips - 2, -1, -1):
+            act(i + (i >= chip).astype(jnp.int32))
+
+    def gather_start(turn, buffer):
         piece = buffer.at[core, chip]
-        return remote(piece, piece, chip_send.at[turn], chip_recv.at[mask - 1], place(mask, core))
-
-    def to_far_side(turn, buffer, mask):
-        piece = buffer.at[core, chip]
-        return remote(piece, piece, side_send.at[turn], side_recv.at[turn], place(mask, other))
-
-    def to_sibling(turn, buffer, mask):
-        piece = buffer.at[core, flipped(chip, mask)]
-        return remote(piece, piece, side_send.at[turn], side_recv.at[turn], sibling)
-
-    direct = ()
-
-    def gather_start(turn, buffer):
-        for mask in range(chips - 1, 0, -1):
-            to_chip(turn, buffer, mask).start()
-            if mask in direct:
-                to_far_side(turn, buffer, mask).start()
-        to_sibling(turn, buffer, 0).start()
+
+        def send_one(peer):
+            remote(
+                piece, piece, chip_send.at[turn], plane_recv.at[shift_of(peer)],
+                seat_of(peer, core),
+            ).start()
+
+        each_peer(turn, send_one)
 
     def gather_finish(turn, buffer):
-        for mask in range(1, chips):
-            piece = buffer.at[core, flipped(chip, mask)]
+        for step in [0,1,3,2]:
+            group = buffer.at[core, pl.ds(0, near if step else near - 1)]
             remote(
-                piece, piece, chip_send.at[turn], chip_recv.at[mask - 1], place(mask, core)
+                group, group, chip_send.at[turn], plane_recv.at[step], sibling
             ).wait_recv()
-            if mask not in direct:
-                to_sibling(turn, buffer, mask).start()
+            to_sibling(turn, buffer, step).start()
         remote(
             buffer.at[other], buffer.at[other], side_send.at[turn], side_recv.at[turn], sibling
         ).wait_recv()
 
     def gather_sent(turn, buffer):
         some = buffer.at[0, pl.ds(0, chips - 1)]
-        remote(some, some, chip_send.at[turn], chip_recv.at[0], sibling).wait_send()
+        remote(some, some, chip_send.at[turn], plane_recv.at[0], sibling).wait_send()
         remote(
             buffer.at[0], buffer.at[0], side_send.at[turn], side_recv.at[turn], sibling
         ).wait_send()
 
     loads["core"].wait()
     parts[core, chip] = core_ref[...].astype(jnp.bfloat16)
-    pl.semaphore_wait(barrier, n - 1)
-    gather_start(0, parts)
-    loads["u_in"].wait()
-    perm = pair_matrix(rank)
-    u_in = dot(perm, uin_ref[...], ((1,), (0,))).astype(jnp.bfloat16)
-    pair_ref[...] = dot(uin_ref[...], perm, ((0,), (1,))).astype(jnp.bfloat16)
-    loads["x"].wait()
-    x = x_ref[...].astype(jnp.float32).reshape(cells, chans).astype(jnp.bfloat16)
-    in_proj = dot(x, u_in, ((1,), (1,))).astype(jnp.bfloat16).astype(jnp.float32)
-    wide_in[1, 1 : frames + 1, 1 : rows + 1] = in_proj.reshape(frames, rows, cols, rank)
-
     def halo_copy(wide, turn, slot):
         dr, dc = NEIGHBOURS[slot]
         inner = slice(1, rows + 1)
@@ -333,7 +325,17 @@
             def _():
                 act(halo_copy(wide, turn, slot))
 
+    loads["u_in"].wait()
+    perm = pair_matrix(rank)
+    u_in = dot(perm, uin_ref[...], ((1,), (0,))).astype(jnp.bfloat16)
+    pair_ref[...] = dot(uin_ref[...], perm, ((0,), (1,))).astype(jnp.bfloat16)
+    loads["x"].wait()
+    x = x_ref[...].astype(jnp.float32).reshape(cells, chans).astype(jnp.bfloat16)
+    in_proj = dot(x, u_in, ((1,), (1,))).astype(jnp.bfloat16).astype(jnp.float32)
+    wide_in[1, 1 : frames + 1, 1 : rows + 1] = in_proj.reshape(frames, rows, cols, rank)
+    pl.semaphore_wait(barrier, n - 1)
     halo_each(wide_in, 0, lambda copy: copy.start(), 1)
+    gather_start(0, parts)
     halo_each(wide_in, 0, lambda copy: copy.wait_recv(), -1)
     fill_taps(wide_in, taps_in, False)
     gather_finish(0, parts)
@@ -371,14 +373,12 @@
             jnp.bfloat16
         )
 
-    def share(mask):
-        return remote(
-            send.at[flipped(chip, mask)], recv.at[chip], chip_send.at[1], sum_recv.at[0],
-            place(mask, core),
-        )
-
-    for mask in range(chips - 1, 0, -1):
-        share(mask).start()
+    def share(peer):
+        remote(
+            send.at[peer], recv.at[chip], chip_send.at[1], sum_recv.at[0], seat_of(peer, core)
+        ).start()
+
+    each_peer(1, share)
     recv[chip] = send[chip]
 
     halo_each(wide_out, 1, lambda copy: copy.wait_recv(), -1)
@@ -420,7 +420,7 @@
 
 
 def build_kernel(
-    group, cube_ref, uin_ref, uout_ref, fg_from, core_from, one_from, two_from,
+    group, run, cube_ref, uin_ref, uout_ref, fg_from, core_from, one_from, two_from,
     out_hbm, fg_to, core_to, one_to, two_to, out_ref, side_sem, out_sem,
 ):
     rank = uin_ref.shape[1]
@@ -432,6 +432,8 @@
     ]
     u_in = uin_ref[...]
     u_out = uout_ref[...]
+    for side in sides:
+        side.start()
     copies = []
     for first in range(0, out_ref.shape[0], group):
         cube = cube_ref[rank * first : rank * (first + group), :]
@@ -439,15 +441,13 @@
         for tap in range(group):
             span = slice(rank * tap, rank * (tap + 1))
             out_ref[first + tap] = dot(u_in, halfway[span], ((1,), (0,))).astype(jnp.bfloat16)
-        block = pl.ds(first, group)
-        copy = pltpu.make_async_copy(
-            out_ref.at[block], out_hbm.at[block], out_sem.at[first // group]
-        )
-        copy.start()
-        copies.append(copy)
-        if first == 0:
-            for side in sides:
-                side.start()
+            if (tap + 1) % run == 0:
+                block = pl.ds(first + tap + 1 - run, run)
+                copy = pltpu.make_async_copy(
+                    out_ref.at[block], out_hbm.at[block], out_sem.at[len(copies)]
+                )
+                copy.start()
+                copies.append(copy)
     for copy in sides + copies:
         copy.wait()
 
@@ -511,7 +511,7 @@
             pltpu.SemaphoreType.DMA((2, 3, sides_of)),
             pltpu.SemaphoreType.DMA((2, 3, sides_of)),
             pltpu.SemaphoreType.DMA((3,)),
-            pltpu.SemaphoreType.DMA((chips - 1,)),
+            pltpu.SemaphoreType.DMA((chips // min(4, chips),)),
             pltpu.SemaphoreType.DMA((1,)),
             pltpu.SemaphoreType.DMA((3,)),
             pltpu.SemaphoreType.DMA((3,)),
@@ -530,9 +530,9 @@
         in_hbm(u_in.T),
         in_hbm(u_out.T),
     )
-    group = 9 if taps % 9 == 0 else 1
+    group, run = (9,3)
     kernel_next, fg, core_next, one_next, two_next = pl.pallas_call(
-        functools.partial(build_kernel, group),
+        functools.partial(build_kernel, group, run),
         out_shape=(
             jax.ShapeDtypeStruct((taps, chans, chans), bf16),
             jax.ShapeDtypeStruct(frames_in.shape, bf16),
@@ -545,7 +545,7 @@
         scratch_shapes=[
             pltpu.VMEM((taps, chans, chans), bf16),
             pltpu.SemaphoreType.DMA((4,)),
-            pltpu.SemaphoreType.DMA((taps // group,)),
+            pltpu.SemaphoreType.DMA((taps // run,)),
         ],
         compiler_params=pltpu.CompilerParams(vmem_limit_bytes=vmem_limit),
         name="build",

time: 30.5 us -> 29.4 us (0.964)
  Pallas kernels: 29.6 us -> 28.5 us
    pallas_call x1, Pallas kernels: 27.1 us -> 26.1 us  [fused_body(): pl.pallas_call(functools.partial(step_kernel, grid_shape, cells * n), out...]
where the time goes in v2:
time: 29.4 us; the launch traced here: 29.2 us
  Pallas kernels  28.5 us (97%)
  between operations  0.64 us (2%)
    pallas_call x1, Pallas kernels, fused_body(): pl.pallas_call(functools.partial(step_kernel, grid_shape, cells * n), out...  26.1 us
    pallas_call x1, Pallas kernels, fused_body(): pl.pallas_call(functools.partial(build_kernel, group, run), out_shape=(ja...  2.41 us

profile of v2, /device:TPU:0, one launch (start us, length us, event | category | flops | bytes accessed | tf_op | source)
XLA Modules:
  0.0 29.2 jit_solution(6366534139973204186)
XLA Ops:
  0.6 26.1 %step.1 = (bf16[3,6,8,256]{3,2,1,0:T(8,128)(2,1)S(1)}, f32[27,128]{1,0:T(8,128)S(1)}, f32[27,128]{1,0:T(8,128)S(1)}, f32[27,128]{1,0:T(8,128)S(1)}, bf16[1728,64...) custom-call(bf16[3,6,8,256]{3,2,1,0:T(8,128)(2,1)} %x_hbm.1, ...), custom_call_target="tpu_custom_call" | custom-call | tf_op jit(solution)/shard_map/step/pallas_call | solution.py:479
  26.8 2.4 %build.1 = (bf16[27,256,256]{2,1,0:T(8,128)(2,1)}, bf16[3,6,8,256]{3,2,1,0:T(8,128)(2,1)}, f32[27,128]{1,0:T(8,128)}, f32[27,128]{1,0:T(8,128)}, f32[27,128]{1,0:T(8,128)}) custom-call(bf16[1728,64]{1,0:T(8,128)(2,1)S(1)} %get-tuple-element.17.cube_ref, bf16[256,64]{1,0:T(8,128)(2,1)S(1)} %get-tuple-element.18.uin_ref, ...), custom_call_target="tpu_custom_call" | custom-call | tf_op jit(solution)/shard_map/build/pallas_call | solution.py:534
